TPU v7x, 32 devices: a whole 2x2x4 slice. The times are simulated.
32 devices in a mesh: head: 4 (over z), ctx: 8 (over y, x, core).
Axes of the slice: x: 2, y: 2, z: 4, core: 2. Of those that a mesh axis runs over, the one named last changes fastest.
Arguments:
- keys: bfloat16 [4096, 5120], P('ctx', 'head'), may hold values from -6 to 6
- queries: bfloat16 [4096, 5120], P('ctx', 'head'), may hold values from -6 to 6
- values: bfloat16 [4096, 5120], P('ctx', 'head'), may hold values from -6 to 6
- rates: float32 [4096, 16], P('ctx', 'head'), may hold values from 0.02 to 1
- gate_fast: float32 [16, 320, 640], P('head'), may hold values from -0.3125 to 0.3125
- up_fast: float32 [16, 320, 640], P('head'), may hold values from -0.3125 to 0.3125
- down_fast: float32 [16, 320, 640], P('head'), may hold values from -0.25 to 0.25
- out_weight: bfloat16 [5120, 5120], P('head'), may hold values from -0.078125 to 0.078125
Outputs:
- layer_out: bfloat16 [4096, 5120], P(('ctx', 'head'))
All inputs are finite; a program needn't handle non-finite values.
Results may differ from a plain program's by a relative error of at most 0.011.
Values sent between devices are 32-bit elements; how exact they have to be, the bound alone decides.
A program may use at most 128 MiB of HBM per device.

v0:
```python
import jax
import jax.numpy as jnp
from jax import lax
from jax.sharding import PartitionSpec as P

NS_STEPS = 5


ns_a = 3.4445
ns_b = -4.775
ns_c = 2.0315
eps_value = 1e-06


def gram_of(iterate):
    return jnp.einsum("...df,...ef->...de", iterate, iterate, precision=lax.Precision.HIGHEST)


def ns_update(iterate, gram):
    square = jnp.einsum("...de,...ef->...df", gram, gram, precision=lax.Precision.HIGHEST)
    mixer = ns_b * gram + ns_c * square
    return ns_a * iterate + jnp.einsum(
        "...de,...ef->...df", mixer, iterate, precision=lax.Precision.HIGHEST
    )


def body(keys, queries, values, rates, gate_fast, up_fast, down_fast, out_weight):
    rows_here = keys.shape[0]
    heads_here = gate_fast.shape[0]
    width = gate_fast.shape[1]
    hidden_width = gate_fast.shape[2]
    key_heads = keys.reshape(rows_here, heads_here, width)
    value_heads = values.reshape(rows_here, heads_here, width)
    query_heads = queries.reshape(rows_here, heads_here, width)
    fast = jnp.stack([gate_fast, up_fast, down_fast])
    fast_b = fast.astype(jnp.bfloat16)
    gate = jnp.einsum("thd,hdf->thf", key_heads, fast_b[0], preferred_element_type=jnp.float32)
    upper = jnp.einsum("thd,hdf->thf", key_heads, fast_b[1], preferred_element_type=jnp.float32)
    sig = jax.nn.sigmoid(gate)
    act = gate * sig
    hidden = (act * upper).astype(jnp.bfloat16)
    dout = (-rates[:, :, None] * value_heads.astype(jnp.float32)).astype(jnp.bfloat16)
    dhid = jnp.einsum("thd,hdf->thf", dout, fast_b[2], preferred_element_type=jnp.float32)
    dgate = (dhid * upper * sig * (1.0 + gate * (1.0 - sig))).astype(jnp.bfloat16)
    dup = (dhid * act).astype(jnp.bfloat16)
    grad_gate = jnp.einsum("thd,thf->hdf", key_heads, dgate, preferred_element_type=jnp.float32)
    grad_up = jnp.einsum("thd,thf->hdf", key_heads, dup, preferred_element_type=jnp.float32)
    grad_down = jnp.einsum("thd,thf->hdf", dout, hidden, preferred_element_type=jnp.float32)
    grads = jnp.stack([grad_gate, grad_up, grad_down])
    matrices = 3 * heads_here
    groups = lax.axis_size("ctx")
    padded_count = -(-matrices // groups) * groups
    flat = grads.reshape(matrices, width, hidden_width)
    filler = jnp.zeros((padded_count - matrices, width, hidden_width), jnp.float32)
    stacked = jnp.concatenate([flat, filler], axis=0)
    owned = lax.psum_scatter(stacked, "ctx", scatter_dimension=0, tiled=True)
    scale = lax.rsqrt(jnp.sum(owned * owned, axis=(-2, -1), keepdims=True) + eps_value)
    owned_iter = owned * scale
    for sweep_index in range(NS_STEPS):
        owned_iter = ns_update(owned_iter, gram_of(owned_iter))
    collected = lax.all_gather(owned_iter, "ctx", axis=0, tiled=True)
    iterate = collected[:matrices].reshape(3, heads_here, width, hidden_width)
    updated = (fast - iterate).astype(jnp.bfloat16)
    query_gate = jnp.einsum(
        "thd,hdf->thf", query_heads, updated[0], preferred_element_type=jnp.float32
    )
    query_up = jnp.einsum(
        "thd,hdf->thf", query_heads, updated[1], preferred_element_type=jnp.float32
    )
    query_hidden = (query_gate * jax.nn.sigmoid(query_gate) * query_up).astype(jnp.bfloat16)
    head_out = jnp.einsum(
        "thf,hdf->thd", query_hidden, updated[2], preferred_element_type=jnp.float32
    )
    joined = head_out.astype(jnp.bfloat16).reshape(rows_here, heads_here * width)
    result = lax.psum_scatter(
        jnp.dot(joined, out_weight, preferred_element_type=jnp.float32),
        "head",
        scatter_dimension=0,
        tiled=True,
    )
    return result.astype(jnp.bfloat16)


def solution(mesh):
    in_specs = (
        P("ctx", "head"),
        P("ctx", "head"),
        P("ctx", "head"),
        P("ctx", "head"),
        P("head", None, None),
        P("head", None, None),
        P("head", None, None),
        P("head", None),
    )
    out_specs = P(("ctx", "head"), None)
    return jax.shard_map(body, mesh=mesh, in_specs=in_specs, out_specs=out_specs, check_vma=False)
```

profile of v0, /device:TPU:0, one launch (start us, length us, event | category | flops | bytes accessed | tf_op | source)
XLA Modules:
  0.0 505.5 jit_solution(9457267308264844654)
XLA Ops:
  6.5 0.0 reduce-scatter.3.cloned.1.call-start
  6.5 1.6 copy.27
  8.1 4.7 fusion
  12.9 0.0 copy-start
  12.9 3.9 fusion.35
  16.8 3.9 fusion.36
  20.7 2.1 copy.26
  22.8 0.0 slice-start
  22.8 3.1 fusion.37
  25.9 0.0 slice-start.1
  25.9 7.9 %fusion.28 = f32[1,4,320,640]{3,2,1,0:T(8,128)} fusion(f32[4,640,512]{2,1,0:T(8,128)} %fusion.36, bf16[512,4,320]{0,2,1:T(8,128)(2,1)S(1)} %bitcast.173, f32[512,4]{0,1:T(4,128)S(1)} %neg.10, f32[4,640,512]{2,1,0:T(8,128)} %fusion.35), kind=kOutput, calls=%fused_computation.34 | convolution fusion | flops 848691200 | bytes 15081472 | tf_op jit(solution)/shard_map/thd,thf->hdf/dot_general | solution.py:48
  33.8 6.6 %fusion.25 = f32[1,4,320,640]{3,2,1,0:T(8,128)} fusion(bf16[512,4,320]{0,2,1:T(8,128)(2,1)S(1)} %bitcast.168, f32[4,640,512]{2,1,0:T(8,128)S(1)} %bitcast.175, f32[4,640,512]{2,1,0:T(8,128)} %fusion.36, f32[4,640,512]{2,1,0:T(8,128)S(1)} %fusion.37), kind=kOutput, calls=%fused_computation.33 | convolution fusion | flops 851968000 | bytes 20316160 | tf_op jit(solution)/shard_map/thd,thf->hdf/dot_general | solution.py:46
  40.4 3.5 fusion.31
  44.0 4.5 pad_maximum_fusion.1
  48.5 5.9 %concatenate.3 = f32[16,320,640]{2,1,0:T(8,128)} pad(f32[12,320,640]{2,1,0:T(8,128)S(1)} %bitcast.158, f32[]{:T(128)} %constant.0.clone.1), padding=0_4x0_0x0_0 | pad | bytes 22937604 | tf_op jit(solution)/shard_map/concatenate | solution.py:55
  54.3 0.0 reduce-scatter.3.cloned.1.call-update
  54.4 0.2 all-gather.2.cloned.1.call-start
  54.6 97.4 %reduce-scatter.3.cloned.1.call-done = f32[2,320,640]{2,1,0:T(8,128)} async-done(((f32[16,320,640]{2,1,0:T(8,128)}), f32[2,320,640]{2,1,0:T(8,128)}) %reduce-scatter.3.cloned.1.call-update) | async-done | bytes 1638416 | tf_op jit(solution)/shard_map/reduce_scatter | solution.py:56
  152.0 1.7 multiply_reduce_fusion
  153.7 5.5 %fusion.41 = f32[2,320,320]{2,1,0:T(8,128)S(1)} fusion(f32[2,320,640]{2,1,0:T(8,128)} %reduce-scatter.3.cloned.1.call-done, f32[2]{0:T(128)S(1)} %add_rsqrt_fusion), kind=kOutput, calls=%fused_computation.53 | convolution fusion | flops 1573273600 | bytes 2457608 | tf_op jit(solution)/shard_map/...df,...ef->...de/dot_general | solution.py:16
  159.2 2.1 fusion.48
  161.3 3.3 multiply_add_fusion.4
  164.6 3.3 fusion.57
  168.0 2.3 fusion.47
  170.3 3.1 multiply_add_fusion.3
  173.4 3.3 fusion.58
  176.7 2.1 fusion.46
  178.8 3.6 multiply_add_fusion.2
  182.5 3.3 fusion.59
  185.8 2.1 fusion.45
  187.9 3.1 multiply_add_fusion.1
  191.0 3.5 fusion.60
  194.5 2.1 fusion.44
  196.6 0.0 copy-start.4
  196.6 4.3 multiply_add_fusion
  201.0 0.0 all-gather.2.cloned.1.call-update
  201.0 0.0 reduce-scatter.5.cloned.1.call-start
  201.0 0.0 copy-done.4
  201.0 1.5 copy.31
  202.5 72.8 %all-gather.2.cloned.1.call-done = f32[16,320,640]{2,1,0:T(8,128)} async-done(((f32[2,320,640]{2,1,0:T(8,128)}), f32[16,320,640]{2,1,0:T(8,128)}) %all-gather.2.cloned.1.call-update) | async-done | bytes 13107216 | tf_op jit(solution)/shard_map/all_gather | solution.py:61
  275.4 8.1 %slice.31 = f32[12,320,640]{2,1,0:T(8,128)} slice(f32[16,320,640]{2,1,0:T(8,128)} %all-gather.2.cloned.1.call-done), slice={[0:12], [0:320], [0:640]} | slice | bytes 19660800 | tf_op jit(solution)/shard_map/slice | solution.py:62
  283.5 9.5 %subtract_convert_fusion = bf16[3,4,320,640]{3,2,1,0:T(8,128)(2,1)} fusion(f32[3,4,320,640]{3,2,1,0:T(8,128)} %bitcast.159, f32[1,4,320,640]{3,2,1,0:T(8,128)S(1)} %bitcast.161, f32[1,4,320,640]{3,2,1,0:T(8,128)} %bitcast.163, f32[1,4,320,640]{3,2,1,0:T(8,128)} %bitcast.165), kind=kLoop, calls=%fused_computation.2 | loop fusion | flops 9830400 | bytes 24576000 | tf_op jit(solution)/shard_map/convert_element_type | solution.py:63
  293.0 5.8 %fusion.34 = f32[4,640,512]{2,1,0:T(8,128)} fusion(bf16[512,4,320]{0,2,1:T(8,128)(2,1)} %bitcast.170, bf16[3,4,320,640]{3,2,1,0:T(8,128)(2,1)} %subtract_convert_fusion), kind=kOutput, calls=%fused_computation.38 | convolution fusion | flops 838860800 | bytes 8192000 | tf_op jit(solution)/shard_map/thd,hdf->thf/dot_general | solution.py:64
  298.8 6.4 %fusion.38 = bf16[4,320,512]{2,1,0:T(8,128)(2,1)S(1)} fusion(f32[4,640,512]{2,1,0:T(8,128)} %fusion.34, bf16[512,4,320]{0,2,1:T(8,128)(2,1)S(1)} %bitcast.171, bf16[3,4,320,640]{3,2,1,0:T(8,128)(2,1)} %subtract_convert_fusion), kind=kOutput, calls=%fused_computation.52 | convolution fusion | flops 1686241280 | bytes 11141120 | tf_op jit(solution)/shard_map/thf,hdf->thd/dot_general | solution.py:71
  305.2 12.4 %fusion.61 = f32[512,5120]{1,0:T(8,128)} fusion(bf16[512,1280]{0,1:T(8,128)(2,1)S(1)} %bitcast.176, bf16[1280,5120]{1,0:T(8,128)(2,1)} %param.15), kind=kOutput, calls=%fused_computation.77 | convolution fusion | flops 6710886400 | bytes 24903680 | tf_op jit(solution)/shard_map/dot_general | solution.py:76
  317.6 0.0 reduce-scatter.5.cloned.1.call-update
  317.6 178.2 %reduce-scatter.5.cloned.1.call-done = f32[128,5120]{1,0:T(8,128)} async-done(((f32[512,5120]{1,0:T(8,128)}), f32[128,5120]{1,0:T(8,128)}) %reduce-scatter.5.cloned.1.call-update) | async-done | bytes 2621456 | tf_op jit(solution)/shard_map/reduce_scatter | solution.py:75
  495.8 3.0 convert_element_type.47
  (14 shorter events, 0.0 us)
Async XLA Ops:
  6.5 145.4 %reduce-scatter.3.cloned.1.call-start = ((), (), s32[]{:S(2)}) async-start(), calls=%async_computation.2 | async-start | bytes 14745600 | tf_op jit(solution)/shard_map/reduce_scatter | solution.py:56
  12.9 3.9 copy-start
  16.8 3.9 copy-start.5
  22.8 11.1 %slice-start = ((s8[5242880]{0:T(1024)(128)(4,1)}), s8[4194304]{0:T(1024)(128)(4,1)S(1)}, s32[]{:S(2)}) async-start(s8[5242880]{0:T(1024)(128)(4,1)} %bitcast.174), calls=%async_computation.5 | async-start | bytes 8388608
  25.9 7.9 %slice-start.1 = ((s8[5242880]{0:T(1024)(128)(4,1)}), s8[1048576]{0:T(1024)(128)(4,1)S(1)}, s32[]{:S(2)}) async-start(s8[5242880]{0:T(1024)(128)(4,1)} %bitcast.174), calls=%async_computation.6 | async-start | bytes 2097152
  54.4 221.0 %all-gather.2.cloned.1.call-start = ((), (), s32[]{:S(2)}) async-start(), calls=%async_computation.3 | async-start | bytes 14745600 | tf_op jit(solution)/shard_map/all_gather | solution.py:61
  153.7 7.6 %copy-start.1 = (f32[2,320,640]{2,1,0:T(8,128)S(1)}, f32[2,320,640]{2,1,0:T(8,128)}, u32[]{:S(2)}) copy-start(f32[2,320,640]{2,1,0:T(8,128)} %reduce-scatter.3.cloned.1.call-done) | copy-start | bytes 4915204
  196.6 4.4 copy-start.4
  201.0 294.8 %reduce-scatter.5.cloned.1.call-start = ((), (), s32[]{:S(2)}) async-start(), calls=%async_computation.4 | async-start | bytes 13107200 | tf_op jit(solution)/shard_map/reduce_scatter | solution.py:75
  202.5 81.0 %copy-start.2 = (f32[4,320,640]{2,1,0:T(8,128)S(1)}, f32[4,320,640]{2,1,0:T(8,128)}, u32[]{:S(2)}) copy-start(f32[4,320,640]{2,1,0:T(8,128)} %param.14) | copy-start | bytes 9830404
  293.0 5.8 %copy-start.3 = (bf16[512,1280]{0,1:T(8,128)(2,1)S(1)}, bf16[512,1280]{0,1:T(8,128)(2,1)}, u32[]{:S(2)}) copy-start(bf16[512,1280]{0,1:T(8,128)(2,1)} %copy.31) | copy-start | bytes 3932164
Sparse Core Ops, SparseCore 0:
  54.5 97.4 reduce-scatter.2
  201.1 74.2 all-gather.1
  317.7 178.0 reduce-scatter.4
where the time goes:
time: 509 us; the launch traced here: 505 us
  waiting for transfers between devices  348 us (68%)
  matrix products  101 us (20%)
  other arithmetic  23.4 us (5%)
  local copies, waits for them, and re-layouts  19.2 us (4%)
  between operations  13.5 us (3%)
    reduce_scatter x1, waiting for transfers between devices, body(): lax.psum_scatter(jnp.dot(joined, out_weight, preferred_element_type=jnp.f...  178 us
    reduce_scatter x1, waiting for transfers between devices, body(): owned = lax.psum_scatter(stacked, 'ctx', scatter_dimension=0, tiled=True)  97.4 us
    all_gather x1, waiting for transfers between devices, body(): collected = lax.all_gather(owned_iter, 'ctx', axis=0, tiled=True)  72.8 us
    dot_general x5, matrix products, gram_of(): jnp.einsum('...df,...ef->...de', iterate, iterate, precision=lax.Precisio...  18.9 us
    dot_general x5, matrix products, ns_update(): jnp.einsum('...de,...ef->...df', mixer, iterate, precision=lax.Precision....  17.5 us
    dot_general x1, matrix products, body(): jnp.dot(joined, out_weight, preferred_element_type=jnp.float32)  12.4 us
    dot_general x5, matrix products, ns_update(): jnp.einsum('...de,...ef->...df', gram, gram, precision=lax.Precision.HIGH...  10.7 us
  transfers between devices with their start and end apart: 3, of which 3 were waited for; matrix products, arithmetic and copies ran while one was open for 0% of the time, Pallas kernels for 0%

commit v1 on v0

--- a/solution.py
+++ b/solution.py
@@ -1,6 +1,10 @@
+import functools
+
 import jax
 import jax.numpy as jnp
 from jax import lax
+from jax.experimental import pallas as pl
+from jax.experimental.pallas import tpu as pltpu
 from jax.sharding import PartitionSpec as P
 
 NS_STEPS = 5
@@ -13,15 +17,103 @@
 
 
 def gram_of(iterate):
-    return jnp.einsum("...df,...ef->...de", iterate, iterate, precision=lax.Precision.HIGHEST)
+    return jnp.einsum("...df,...ef->...de", iterate, iterate, precision=lax.Precision.HIGH)
 
 
 def ns_update(iterate, gram):
-    square = jnp.einsum("...de,...ef->...df", gram, gram, precision=lax.Precision.HIGHEST)
+    square = jnp.einsum("...de,...ef->...df", gram, gram, precision=lax.Precision.HIGH)
     mixer = ns_b * gram + ns_c * square
     return ns_a * iterate + jnp.einsum(
-        "...de,...ef->...df", mixer, iterate, precision=lax.Precision.HIGHEST
+        "...de,...ef->...df", mixer, iterate, precision=lax.Precision.HIGH
     )
+
+
+def out_kernel(n, nsub, x_ref, w_hbm, o_ref, w_ref, send_buf, recv_buf, w_sem, send_sem, recv_sem):
+    me = lax.axis_index("head")
+    right, left = lax.rem(me + 1, n), lax.rem(me + n - 1, n)
+    neighbours = (right, left)
+    rows = x_ref.shape[0] // n
+    half = w_ref.shape[1] // 2
+    sub = half // nsub
+
+    def columns(way, j):
+        return pl.ds(way * half + j * sub, sub)
+
+    loads = {}
+    for j in range(nsub):
+        for way in range(2):
+            loads[way, j] = pltpu.make_async_copy(
+                w_hbm.at[:, columns(way, j)], w_ref.at[:, columns(way, j)], w_sem.at[way, j]
+            )
+            loads[way, j].start()
+
+    barrier = pltpu.get_barrier_semaphore()
+    for neighbour in neighbours:
+        pl.semaphore_signal(
+            barrier, inc=1, device_id={"head": neighbour}, device_id_type=pl.DeviceIdType.MESH
+        )
+    pl.semaphore_wait(barrier, 2)
+
+    def part(dest, way, j):
+        block = x_ref[pl.ds(pl.multiple_of(dest * rows, rows), rows), :]
+        return jnp.dot(block, w_ref[:, columns(way, j)], preferred_element_type=jnp.float32)
+
+    copies = {}
+    for s in range(n - 1):
+        dests = (lax.rem(me + 2 * n - 1 - s, n), lax.rem(me + 1 + s, n))
+        for j in range(nsub):
+            for way in range(2):
+                if s == 0:
+                    loads[way, j].wait()
+                total = part(dests[way], way, j)
+                if s > 0:
+                    copies[way, s - 1, j].wait_recv()
+                    total = total + recv_buf[way, s - 1, j]
+                send_buf[way, s, j] = total
+                copy = pltpu.make_async_remote_copy(
+                    src_ref=send_buf.at[way, s, j],
+                    dst_ref=recv_buf.at[way, s, j],
+                    send_sem=send_sem.at[way, s, j],
+                    recv_sem=recv_sem.at[way, s, j],
+                    device_id={"head": neighbours[way]},
+                    device_id_type=pl.DeviceIdType.MESH,
+                )
+                copy.start()
+                copies[way, s, j] = copy
+    for j in range(nsub):
+        for way in range(2):
+            total = part(me, way, j)
+            if n > 1:
+                copies[way, n - 2, j].wait_recv()
+                total = total + recv_buf[way, n - 2, j]
+            o_ref[:, columns(way, j)] = total.astype(o_ref.dtype)
+    for copy in copies.values():
+        copy.wait_send()
+
+
+def project(joined, out_weight):
+    n = lax.axis_size("head")
+    tokens, depth = joined.shape
+    cols = out_weight.shape[1]
+    nsub = 4
+    rows = tokens // n
+    slots = (2, n - 1, nsub, rows, cols // (2 * nsub))
+    return pl.pallas_call(
+        functools.partial(out_kernel, n, nsub),
+        out_shape=jax.ShapeDtypeStruct((rows, cols), jnp.bfloat16),
+        in_specs=[pl.BlockSpec(memory_space=pltpu.VMEM), pl.BlockSpec(memory_space=pl.ANY)],
+        out_specs=pl.BlockSpec(memory_space=pltpu.VMEM),
+        scratch_shapes=[
+            pltpu.VMEM((depth, cols), jnp.bfloat16),
+            pltpu.VMEM(slots, jnp.float32),
+            pltpu.VMEM(slots, jnp.float32),
+            pltpu.SemaphoreType.DMA((2, nsub)),
+            pltpu.SemaphoreType.DMA((2, n - 1, nsub)),
+            pltpu.SemaphoreType.DMA((2, n - 1, nsub)),
+        ],
+        compiler_params=pltpu.CompilerParams(collective_id=0, has_side_effects=True),
+        name="project",
+    )(joined, out_weight)
 
 
 def body(keys, queries, values, rates, gate_fast, up_fast, down_fast, out_weight):
@@ -72,13 +164,7 @@
         "thf,hdf->thd", query_hidden, updated[2], preferred_element_type=jnp.float32
     )
     joined = head_out.astype(jnp.bfloat16).reshape(rows_here, heads_here * width)
-    result = lax.psum_scatter(
-        jnp.dot(joined, out_weight, preferred_element_type=jnp.float32),
-        "head",
-        scatter_dimension=0,
-        tiled=True,
-    )
-    return result.astype(jnp.bfloat16)
+    return project(joined, out_weight)
 
 
 def solution(mesh):

time: 509 us -> 477 us (0.937)
  waiting for transfers between devices: 348 us -> 170 us
  Pallas kernels: 0 us -> 177 us
  matrix products: 101 us -> 67.8 us
    reduce_scatter x1 -> x0, waiting for transfers between devices: 178 us -> none  [body(): lax.psum_scatter(jnp.dot(joined, out_weight, preferred_element_type=jnp.f...]
    pallas_call x0 -> x1, Pallas kernels: none -> 177 us  [project(): pl.pallas_call(functools.partial(out_kernel, n, nsub), out_shape=jax.Shap...]
    dot_general x6 -> x5, matrix products: 23.1 us -> 5.9 us  [ns_update(): jnp.einsum('...de,...ef->...df', gram, gram, precision=lax.Precision.HIGH)]
    dot_general x5, matrix products: 18.9 us -> 10.6 us  [gram_of(): jnp.einsum('...df,...ef->...de', iterate, iterate, precision=lax.Precisio...]
    dot_general x5, matrix products: 17.5 us -> 10.2 us  [ns_update(): jnp.einsum('...de,...ef->...df', mixer, iterate, precision=lax.Precision....]
  transfers between devices with their start and end apart: 3 -> 2, of which waited for: 3 -> 2; matrix products, arithmetic and copies ran while one was open for 0% -> 0% of each run, Pallas kernels for 0% -> 0%
where the time goes in v1:
time: 477 us; the launch traced here: 473 us
  Pallas kernels  177 us (37%)
  waiting for transfers between devices  170 us (36%)
  matrix products  67.8 us (14%)
  local copies, waits for them, and re-layouts  23 us (5%)
  other arithmetic  20.5 us (4%)
  between operations  14.1 us (3%)
    pallas_call x1, Pallas kernels, project(): pl.pallas_call(functools.partial(out_kernel, n, nsub), out_shape=jax.Shap...  177 us
    reduce_scatter x1, waiting for transfers between devices, body(): owned = lax.psum_scatter(stacked, 'ctx', scatter_dimension=0, tiled=True)  97.1 us
    all_gather x1, waiting for transfers between devices, body(): collected = lax.all_gather(owned_iter, 'ctx', axis=0, tiled=True)  72.9 us
    dot_general x5, matrix products, gram_of(): jnp.einsum('...df,...ef->...de', iterate, iterate, precision=lax.Precisio...  10.6 us
    dot_general x5, matrix products, ns_update(): jnp.einsum('...de,...ef->...df', mixer, iterate, precision=lax.Precision....  10.2 us
  transfers between devices with their start and end apart: 2, of which 2 were waited for; matrix products, arithmetic and copies ran while one was open for 0% of the time, Pallas kernels for 0%

profile of v1, /device:TPU:0, one launch (start us, length us, event | category | flops | bytes accessed | tf_op | source)
XLA Modules:
  0.0 472.8 jit_solution(8641707590590347823)
XLA Ops:
  6.5 0.0 reduce-scatter.2.cloned.1.call-start
  6.5 1.6 copy.29
  8.1 4.7 %fusion = bf16[3,4,320,640]{3,2,1,0:T(8,128)(2,1)S(1)} fusion(f32[1,4,320,640]{3,2,1,0:T(8,128)} %bitcast.158, f32[1,4,320,640]{3,2,1,0:T(8,128)} %bitcast.160, f32[1,4,320,640]{3,2,1,0:T(8,128)} %bitcast.162), kind=kLoop, calls=%fused_computation.3 | loop fusion | flops 4915200 | bytes 14745600 | tf_op jit(solution)/shard_map/convert_element_type | solution.py:128
  12.9 0.0 copy-start
  12.9 3.9 fusion.35
  16.8 0.0 copy-done
  16.8 3.9 fusion.36
  20.7 0.0 copy-done.5
  20.7 1.8 copy.28
  22.5 0.0 slice-start
  22.5 3.1 fusion.37
  25.7 0.0 slice-start.1
  25.7 7.9 %fusion.28 = f32[1,4,320,640]{3,2,1,0:T(8,128)} fusion(f32[4,640,512]{2,1,0:T(8,128)} %fusion.36, bf16[512,4,320]{0,2,1:T(8,128)(2,1)S(1)} %bitcast.171, f32[512,4]{0,1:T(4,128)S(1)} %neg.10, f32[4,640,512]{2,1,0:T(8,128)} %fusion.35), kind=kOutput, calls=%fused_computation.34 | convolution fusion | flops 848691200 | bytes 15081472 | tf_op jit(solution)/shard_map/thd,thf->hdf/dot_general | solution.py:140
  33.6 0.0 slice-done
  33.6 6.6 %fusion.25 = f32[1,4,320,640]{3,2,1,0:T(8,128)} fusion(bf16[512,4,320]{0,2,1:T(8,128)(2,1)S(1)} %bitcast.166, f32[4,640,512]{2,1,0:T(8,128)S(1)} %bitcast.173, f32[4,640,512]{2,1,0:T(8,128)} %fusion.36, f32[4,640,512]{2,1,0:T(8,128)S(1)} %fusion.37), kind=kOutput, calls=%fused_computation.33 | convolution fusion | flops 851968000 | bytes 20316160 | tf_op jit(solution)/shard_map/thd,thf->hdf/dot_general | solution.py:138
  40.2 3.5 fusion.31
  43.7 4.5 pad_maximum_fusion.1
  48.2 5.9 %concatenate.3 = f32[16,320,640]{2,1,0:T(8,128)} pad(f32[12,320,640]{2,1,0:T(8,128)S(1)} %bitcast.156, f32[]{:T(128)} %constant.0.clone.1), padding=0_4x0_0x0_0 | pad | bytes 22937604 | tf_op jit(solution)/shard_map/concatenate | solution.py:147
  54.1 0.0 reduce-scatter.2.cloned.1.call-update
  54.1 0.5 all-gather.2.cloned.1.call-start
  54.6 97.1 %reduce-scatter.2.cloned.1.call-done = f32[2,320,640]{2,1,0:T(8,128)} async-done(((f32[16,320,640]{2,1,0:T(8,128)}), f32[2,320,640]{2,1,0:T(8,128)}) %reduce-scatter.2.cloned.1.call-update) | async-done | bytes 1638416 | tf_op jit(solution)/shard_map/reduce_scatter | solution.py:148
  151.7 1.7 multiply_reduce_fusion
  153.5 3.8 fusion.41
  157.3 1.2 fusion.48
  158.5 1.8 multiply_add_fusion.4
  160.3 1.7 fusion.57
  162.0 1.2 fusion.47
  163.2 1.8 multiply_add_fusion.3
  164.9 1.7 fusion.58
  166.6 1.2 fusion.46
  167.8 1.9 multiply_add_fusion.2
  169.8 1.7 fusion.59
  171.5 1.2 fusion.45
  172.6 1.8 multiply_add_fusion.1
  174.4 1.7 fusion.60
  176.1 1.2 fusion.44
  177.3 0.0 copy-start.4
  177.3 2.9 multiply_add_fusion
  180.2 0.0 all-gather.2.cloned.1.call-update
  180.3 1.5 copy.33
  181.8 72.9 %all-gather.2.cloned.1.call-done = f32[16,320,640]{2,1,0:T(8,128)} async-done(((f32[2,320,640]{2,1,0:T(8,128)}), f32[16,320,640]{2,1,0:T(8,128)}) %all-gather.2.cloned.1.call-update) | async-done | bytes 13107216 | tf_op jit(solution)/shard_map/all_gather | solution.py:153
  254.6 8.1 %slice.31 = f32[12,320,640]{2,1,0:T(8,128)} slice(f32[16,320,640]{2,1,0:T(8,128)} %all-gather.2.cloned.1.call-done), slice={[0:12], [0:320], [0:640]} | slice | bytes 19660800 | tf_op jit(solution)/shard_map/slice | solution.py:154
  262.8 9.5 %subtract_convert_fusion = bf16[3,4,320,640]{3,2,1,0:T(8,128)(2,1)} fusion(f32[3,4,320,640]{3,2,1,0:T(8,128)} %bitcast.157, f32[1,4,320,640]{3,2,1,0:T(8,128)S(1)} %bitcast.159, f32[1,4,320,640]{3,2,1,0:T(8,128)} %bitcast.161, f32[1,4,320,640]{3,2,1,0:T(8,128)} %bitcast.163), kind=kLoop, calls=%fused_computation.2 | loop fusion | flops 9830400 | bytes 24576000 | tf_op jit(solution)/shard_map/convert_element_type | solution.py:155
  272.3 5.8 %fusion.34 = f32[4,640,512]{2,1,0:T(8,128)} fusion(bf16[512,4,320]{0,2,1:T(8,128)(2,1)} %bitcast.168, bf16[3,4,320,640]{3,2,1,0:T(8,128)(2,1)} %subtract_convert_fusion), kind=kOutput, calls=%fused_computation.38 | convolution fusion | flops 838860800 | bytes 8192000 | tf_op jit(solution)/shard_map/thd,hdf->thf/dot_general | solution.py:156
  278.1 6.4 %fusion.38 = bf16[4,320,512]{2,1,0:T(8,128)(2,1)S(1)} fusion(f32[4,640,512]{2,1,0:T(8,128)} %fusion.34, bf16[512,4,320]{0,2,1:T(8,128)(2,1)S(1)} %bitcast.169, bf16[3,4,320,640]{3,2,1,0:T(8,128)(2,1)} %subtract_convert_fusion), kind=kOutput, calls=%fused_computation.52 | convolution fusion | flops 1686241280 | bytes 11141120 | tf_op jit(solution)/shard_map/thf,hdf->thd/dot_general | solution.py:163
  284.5 1.6 copy.35.x_ref
  286.1 176.9 %project.1 = bf16[128,5120]{1,0:T(8,128)(2,1)} custom-call(bf16[512,1280]{1,0:T(8,128)(2,1)} %copy.35.x_ref, bf16[1280,5120]{1,0:T(8,128)(2,1)} %w_hbm.1), custom_call_target="tpu_custom_call" | custom-call | tf_op jit(solution)/shard_map/project/pallas_call | solution.py:101
  463.0 2.5 copy.41
  (12 shorter events, 0.0 us)
Async XLA Ops:
  6.5 145.2 %reduce-scatter.2.cloned.1.call-start = ((), (), s32[]{:S(2)}) async-start(), calls=%async_computation.1 | async-start | bytes 14745600 | tf_op jit(solution)/shard_map/reduce_scatter | solution.py:148
  12.9 3.9 copy-start
  16.8 3.9 copy-start.5
  22.5 11.1 %slice-start = ((s8[5242880]{0:T(1024)(128)(4,1)}), s8[4194304]{0:T(1024)(128)(4,1)S(1)}, s32[]{:S(2)}) async-start(s8[5242880]{0:T(1024)(128)(4,1)} %bitcast.172), calls=%async_computation.3 | async-start | bytes 8388608
  25.7 7.9 %slice-start.1 = ((s8[5242880]{0:T(1024)(128)(4,1)}), s8[1048576]{0:T(1024)(128)(4,1)S(1)}, s32[]{:S(2)}) async-start(s8[5242880]{0:T(1024)(128)(4,1)} %bitcast.172), calls=%async_computation.4 | async-start | bytes 2097152
  54.1 200.5 %all-gather.2.cloned.1.call-start = ((), (), s32[]{:S(2)}) async-start(), calls=%async_computation.2 | async-start | bytes 14745600 | tf_op jit(solution)/shard_map/all_gather | solution.py:153
  153.5 5.0 %copy-start.1 = (f32[2,320,640]{2,1,0:T(8,128)S(1)}, f32[2,320,640]{2,1,0:T(8,128)}, u32[]{:S(2)}) copy-start(f32[2,320,640]{2,1,0:T(8,128)} %reduce-scatter.2.cloned.1.call-done) | copy-start | bytes 4915204
  177.3 3.0 copy-start.4
  181.7 81.0 %copy-start.2 = (f32[4,320,640]{2,1,0:T(8,128)S(1)}, f32[4,320,640]{2,1,0:T(8,128)}, u32[]{:S(2)}) copy-start(f32[4,320,640]{2,1,0:T(8,128)} %param.14) | copy-start | bytes 9830404
  272.3 5.8 %copy-start.3 = (bf16[512,1280]{0,1:T(8,128)(2,1)S(1)}, bf16[512,1280]{0,1:T(8,128)(2,1)}, u32[]{:S(2)}) copy-start(bf16[512,1280]{0,1:T(8,128)(2,1)} %copy.33) | copy-start | bytes 3932164
Sparse Core Ops, SparseCore 0:
  54.2 97.4 reduce-scatter.1
  180.4 74.2 all-gather.1
